TPU v7x, 32 devices: a whole 2x2x4 slice. The times are simulated.
32 devices in a mesh: dp: 8 (over y, x, core), mp: 4 (over z).
Axes of the slice: x: 2, y: 2, z: 4, core: 2. Of those that a mesh axis runs over, the one named last changes fastest.
Arguments:
- tokens: bfloat16 [8192, 2048], P(('dp', 'mp')), may hold values from -6 to 6
- valid: int32 [8], P('dp'), may hold values from 256 to 1024, as said below
- attn_gain: float32 [2048], replicated, may hold values from 0.25 to 1.75
- w_query: bfloat16 [2048, 2048], replicated, may hold values from -0.125 to 0.125
- w_key: bfloat16 [2048, 2048], replicated, may hold values from -0.125 to 0.125
- w_value: bfloat16 [2048, 2048], replicated, may hold values from -0.125 to 0.125
- w_rank: bfloat16 [2048, 16], replicated, may hold values from -0.125 to 0.125
- w_forget: bfloat16 [16, 256], replicated, may hold values from -1.5 to 1.5
- forget_bias: float32 [256], replicated, may hold values from -2 to 6
- head_gain: float32 [512], replicated, may hold values from 0.25 to 1.75
- w_out: bfloat16 [2048, 2048], replicated, may hold values from -0.125 to 0.125
- mlp_gain: float32 [2048], replicated, may hold values from 0.25 to 1.75
- w_gate: bfloat16 [2048, 5632], P(None, 'mp'), may hold values from -0.125 to 0.125
- w_up: bfloat16 [2048, 5632], P(None, 'mp'), may hold values from -0.125 to 0.125
- w_down: bfloat16 [5632, 2048], P('mp'), may hold values from -0.15625 to 0.15625
- cotangent: bfloat16 [8192, 2048], P(('dp', 'mp')), may hold values from -6 to 6
Outputs:
- output: bfloat16 [8192, 2048], P(('dp', 'mp'))
- grad_tokens: float32 [8192, 2048], P(('dp', 'mp'))
- grad_attn_gain: float32 [2048], P('dp')
- grad_query: float32 [2048, 2048], P('dp', 'mp')
- grad_key: float32 [2048, 2048], P('dp', 'mp')
- grad_value: float32 [2048, 2048], P('dp', 'mp')
- grad_rank: float32 [2048, 16], P('dp')
- grad_forget: float32 [16, 256], P(None, 'dp')
- grad_forget_bias: float32 [256], P('dp')
- grad_head_gain: float32 [512], P('dp')
- grad_out: float32 [2048, 2048], P('dp', 'mp')
- grad_mlp_gain: float32 [2048], P('dp')
- grad_gate: float32 [2048, 5632], P('dp', 'mp')
- grad_up: float32 [2048, 5632], P('dp', 'mp')
- grad_down: float32 [5632, 2048], P('mp', 'dp')
Inputs may be any that keep to these rules, and one draw needn't show every extreme that they name: Each bucket holds one sequence whose first valid tokens count; one bucket is full in every draw.
All inputs are finite; a program needn't handle non-finite values.
Results may differ from a plain program's by a relative error of at most 0.018.
Values may be sent and summed in bfloat16 or wider, within the bound.
No kernel may reach another device: no remote copies, remote signals or barrier semaphores. Data moves between devices by JAX's collectives and lax.ppermute only.
A program may use at most 448 MiB of HBM per device.

v0:
```python
import math

import jax
import jax.numpy as jnp
from jax import lax
from jax.sharding import PartitionSpec as P

HEADS = 4
BLOCK = 128


EPS = 1e-06
GATE_NORM = 8.0
HIGH_PRECISION = lax.Precision.HIGHEST
CONTRACT_ROWS = (((0,), (0,)), ((), ()))
CONTRACT_COLS = (((1,), (1,)), ((), ()))


def rms_norm(values, gain):
    return values * lax.rsqrt(jnp.mean(values * values, axis=-1, keepdims=True) + EPS) * gain


def silu_slope(raw):
    sigmoid = jax.nn.sigmoid(raw)
    return sigmoid * (1.0 + raw * (1.0 - sigmoid))


def rows_product(left, right):
    return lax.dot_general(left, right, CONTRACT_ROWS, preferred_element_type=jnp.float32)


def cols_product(left, right):
    return lax.dot_general(left, right, CONTRACT_COLS, preferred_element_type=jnp.float32)


def piece_step(states, block):
    key_slot_state, value_slot_state = states
    query_rows, key_row_block, value_row_block, log_decay = block
    length = query_rows.shape[0]
    scale = 1.0 / math.sqrt(query_rows.shape[2])
    running_total = jnp.cumsum(log_decay, axis=0)
    fresh = 1.0 - jnp.exp(log_decay)
    causal = (jnp.arange(length)[:, None] >= jnp.arange(length)[None, :])[:, :, None, None]
    spread = running_total[:, None] - running_total[None, :]
    weights = jnp.where(causal, jnp.exp(jnp.where(causal, spread, 0.0)), 0.0) * fresh[None]
    direct = jnp.einsum("thd,jhd->htj", query_rows, key_row_block, precision=HIGH_PRECISION)
    attention_scores = jnp.exp(running_total) * jnp.einsum(
        "cso,sio->csi", query_rows, key_slot_state, precision=HIGH_PRECISION
    )
    attention_scores = (
        attention_scores + jnp.einsum("htj,tjhm->thm", direct, weights, precision=HIGH_PRECISION)
    ) * scale
    attention_probabilities = jax.nn.softmax(attention_scores, axis=-1)
    mixing = jnp.einsum("thm,tjhm->htj", attention_probabilities, weights, precision=HIGH_PRECISION)
    output_rows = jnp.einsum(
        "lwe,wez->lwz",
        attention_probabilities * jnp.exp(running_total),
        value_slot_state,
        precision=HIGH_PRECISION,
    )
    output_rows = output_rows + jnp.einsum(
        "htj,jhd->thd", mixing, value_row_block, precision=HIGH_PRECISION
    )
    final = running_total[-1]
    carried_state = jnp.exp(final[None] - running_total) * fresh
    key_slot_state = jnp.exp(final)[:, :, None] * key_slot_state + jnp.einsum(
        "eoq,eon->oqn", carried_state, key_row_block, precision=HIGH_PRECISION
    )
    value_slot_state = jnp.exp(final)[:, :, None] * value_slot_state + jnp.einsum(
        "eoq,eon->oqn", carried_state, value_row_block, precision=HIGH_PRECISION
    )
    return ((key_slot_state, value_slot_state), output_rows)


def slot_block(states, block):
    length = block[0].shape[0]
    piece_length = min(16, length)
    count = length // piece_length
    pieces = tuple((member.reshape((count, piece_length) + member.shape[1:]) for member in block))
    states, output_rows = lax.scan(piece_step, states, pieces)
    return (states, output_rows.reshape(block[0].shape))


def slot_mixer(query_rows, key_row_block, value_row_block, log_decay):
    steps = query_rows.shape[0] // BLOCK
    blocks = tuple(
        (
            member.reshape((steps, BLOCK) + member.shape[1:])
            for member in (query_rows, key_row_block, value_row_block, log_decay)
        )
    )
    blank_state = jnp.zeros(
        (query_rows.shape[1], log_decay.shape[2], query_rows.shape[2]), jnp.float32
    )
    _, output_rows = lax.scan(jax.checkpoint(slot_block), (blank_state, blank_state), blocks)
    return output_rows.reshape(query_rows.shape)


def local(
    tokens,
    valid,
    attn_gain,
    w_query,
    w_key,
    w_value,
    w_rank,
    w_forget,
    forget_bias,
    head_gain,
    w_out,
    mlp_gain,
    w_gate,
    w_up,
    w_down,
    cotangent,
):
    shard_rows = tokens.shape[0]
    gathered, upstream = (
        lax.all_gather(tokens, "mp", axis=0, tiled=True),
        lax.all_gather(cotangent, "mp", axis=0, tiled=True),
    )
    group_len = gathered.shape[0]
    model_width = w_query.shape[0]
    head_size = model_width // HEADS
    slot_count = forget_bias.shape[0] // HEADS
    shard_index = lax.axis_index("mp")
    column_width = model_width // lax.axis_size("mp")
    own_begin = shard_index * shard_rows
    valid_mask = (jnp.arange(group_len) < valid[0]).astype(jnp.float32)[:, None]
    resid = gathered.astype(jnp.float32)
    normed, pull_first = jax.vjp(rms_norm, resid, attn_gain)
    normed_low = normed.astype(jnp.bfloat16)
    query_raw = jnp.dot(normed_low, w_query, preferred_element_type=jnp.float32)
    key_raw = jnp.dot(normed_low, w_key, preferred_element_type=jnp.float32)
    value_raw = jnp.dot(normed_low, w_value, preferred_element_type=jnp.float32)
    rank_rows = jnp.dot(normed_low, w_rank, preferred_element_type=jnp.float32)
    forget_dense = w_forget.astype(jnp.float32)
    logits = jnp.dot(rank_rows, forget_dense, precision=HIGH_PRECISION) + forget_bias
    log_decay = jax.nn.log_sigmoid(logits) / GATE_NORM

    def heads_view(values, inner_width):
        return values.astype(jnp.float32).reshape(group_len, HEADS, inner_width)

    mixed, pull_slots = jax.vjp(
        slot_mixer,
        heads_view(jax.nn.silu(query_raw).astype(jnp.bfloat16), head_size),
        heads_view(jax.nn.silu(key_raw).astype(jnp.bfloat16), head_size),
        heads_view(value_raw.astype(jnp.bfloat16), head_size),
        heads_view(log_decay, slot_count),
    )
    head_normed, pull_head = jax.vjp(rms_norm, mixed, head_gain)
    head_low = head_normed.reshape(group_len, model_width).astype(jnp.bfloat16)
    hidden_res = resid + jnp.dot(head_low, w_out, preferred_element_type=jnp.float32)
    normed_mlp, pull_second = jax.vjp(rms_norm, hidden_res, mlp_gain)
    mlp_low = normed_mlp.astype(jnp.bfloat16)
    gate_pre = jnp.dot(mlp_low, w_gate, preferred_element_type=jnp.float32)
    up_pre = jnp.dot(mlp_low, w_up, preferred_element_type=jnp.float32)
    activated = jax.nn.silu(gate_pre)
    inner_low = (activated * up_pre).astype(jnp.bfloat16)
    mlp_own = lax.psum_scatter(
        jnp.dot(inner_low, w_down, preferred_element_type=jnp.float32).astype(jnp.bfloat16),
        "mp",
        scatter_dimension=0,
        tiled=True,
    ).astype(jnp.float32)
    own_mask = lax.dynamic_slice_in_dim(valid_mask, own_begin, shard_rows, 0)
    own_hidden = lax.dynamic_slice_in_dim(hidden_res, own_begin, shard_rows, 0)
    output = ((own_hidden + mlp_own) * own_mask).astype(jnp.bfloat16)
    grad_output = upstream.astype(jnp.float32) * valid_mask
    grad_out_low = grad_output.astype(jnp.bfloat16)
    grad_down = rows_product(inner_low, grad_out_low)
    grad_inner = cols_product(grad_out_low, w_down)
    grad_gate_low = (grad_inner * up_pre * silu_slope(gate_pre)).astype(jnp.bfloat16)
    grad_up_low = (grad_inner * activated).astype(jnp.bfloat16)
    grad_gate = rows_product(mlp_low, grad_gate_low)
    grad_up = rows_product(mlp_low, grad_up_low)
    partial_grad = cols_product(grad_gate_low, w_gate) + cols_product(grad_up_low, w_up)
    grad_normed_mlp = lax.psum(partial_grad, "mp")
    grad_res_mlp, grad_mlp_gain = pull_second(grad_normed_mlp)
    grad_hidden = grad_output + grad_res_mlp

    def own_columns(values):
        return lax.dynamic_slice_in_dim(values, shard_index * column_width, column_width, 1)

    grad_hidden_low = grad_hidden.astype(jnp.bfloat16)
    grad_wout = rows_product(head_low, own_columns(grad_hidden_low))
    grad_head_flat = cols_product(grad_hidden_low, w_out)
    grad_mixed, grad_head_gain = pull_head(grad_head_flat.reshape(group_len, HEADS, head_size))
    grad_query_in, grad_key_in, grad_value_in, grad_log_in = pull_slots(grad_mixed)
    grad_query_low = (grad_query_in.reshape(group_len, model_width) * silu_slope(query_raw)).astype(
        jnp.bfloat16
    )
    grad_key_low = (grad_key_in.reshape(group_len, model_width) * silu_slope(key_raw)).astype(
        jnp.bfloat16
    )
    grad_value_low = grad_value_in.reshape(group_len, model_width).astype(jnp.bfloat16)
    grad_logits = (
        grad_log_in.reshape(group_len, HEADS * slot_count) * jax.nn.sigmoid(-logits) / GATE_NORM
    )
    grad_bias = jnp.sum(grad_logits, axis=0)
    grad_forget = lax.dot_general(
        rank_rows,
        grad_logits,
        CONTRACT_ROWS,
        precision=HIGH_PRECISION,
        preferred_element_type=jnp.float32,
    )
    grad_rank_low = lax.dot_general(
        grad_logits,
        forget_dense,
        CONTRACT_COLS,
        precision=HIGH_PRECISION,
        preferred_element_type=jnp.float32,
    ).astype(jnp.bfloat16)
    grad_wrank = rows_product(normed_low, grad_rank_low)
    grad_wquery = rows_product(normed_low, own_columns(grad_query_low))
    grad_wkey = rows_product(normed_low, own_columns(grad_key_low))
    grad_wvalue = rows_product(normed_low, own_columns(grad_value_low))
    grad_normed = cols_product(grad_query_low, w_query) + cols_product(grad_key_low, w_key)
    grad_normed = (
        grad_normed + cols_product(grad_value_low, w_value) + cols_product(grad_rank_low, w_rank)
    )
    grad_resid, grad_attn_gain = pull_first(grad_normed)
    grad_tokens = lax.dynamic_slice_in_dim(grad_hidden + grad_resid, own_begin, shard_rows, 0)
    (
        sum_query,
        sum_key,
        sum_value,
        sum_rank,
        sum_forget,
        sum_bias,
        sum_head_gain,
        sum_wout,
        sum_attn_gain,
        sum_gate,
        sum_up,
        sum_down,
        sum_mlp_gain,
    ) = (
        lax.psum_scatter(grad_wquery, "dp", scatter_dimension=0, tiled=True),
        lax.psum_scatter(grad_wkey, "dp", scatter_dimension=0, tiled=True),
        lax.psum_scatter(grad_wvalue, "dp", scatter_dimension=0, tiled=True),
        lax.psum_scatter(grad_wrank, "dp", scatter_dimension=0, tiled=True),
        lax.psum_scatter(grad_forget, "dp", scatter_dimension=1, tiled=True),
        lax.psum_scatter(grad_bias, "dp", scatter_dimension=0, tiled=True),
        lax.psum_scatter(grad_head_gain, "dp", scatter_dimension=0, tiled=True),
        lax.psum_scatter(grad_wout, "dp", scatter_dimension=0, tiled=True),
        lax.psum_scatter(grad_attn_gain, "dp", scatter_dimension=0, tiled=True),
        lax.psum_scatter(grad_gate, "dp", scatter_dimension=0, tiled=True),
        lax.psum_scatter(grad_up, "dp", scatter_dimension=0, tiled=True),
        lax.psum_scatter(grad_down, "dp", scatter_dimension=1, tiled=True),
        lax.psum_scatter(grad_mlp_gain, "dp", scatter_dimension=0, tiled=True),
    )
    return (
        output,
        grad_tokens,
        sum_attn_gain,
        sum_query,
        sum_key,
        sum_value,
        sum_rank,
        sum_forget,
        sum_bias,
        sum_head_gain,
        sum_wout,
        sum_mlp_gain,
        sum_gate,
        sum_up,
        sum_down,
    )


def solution(mesh):
    return jax.shard_map(
        local,
        mesh=mesh,
        in_specs=(
            P(("dp", "mp"), None),
            P("dp"),
            P(),
            P(),
            P(),
            P(),
            P(),
            P(),
            P(),
            P(),
            P(),
            P(),
            P(None, "mp"),
            P(None, "mp"),
            P("mp", None),
            P(("dp", "mp"), None),
        ),
        out_specs=(
            P(("dp", "mp"), None),
            P(("dp", "mp"), None),
            P("dp"),
            P("dp", "mp"),
            P("dp", "mp"),
            P("dp", "mp"),
            P("dp", None),
            P(None, "dp"),
            P("dp"),
            P("dp"),
            P("dp", "mp"),
            P("dp"),
            P("dp", "mp"),
            P("dp", "mp"),
            P("mp", "dp"),
        ),
        check_vma=False,
    )
```

profile of v0, /device:TPU:0, one launch (start us, length us, event | category | flops | bytes accessed | tf_op | source)
XLA Modules:
  0.0 5010.8 jit_solution(17685367575077738761)
XLA Ops:
  11.3 81.7 %all-gather.3.cloned.1.call-done = bf16[1024,2048]{1,0:T(8,128)(2,1)} async-done(((bf16[256,2048]{1,0:T(8,128)(2,1)}), bf16[1024,2048]{1,0:T(8,128)(2,1)}) %all-gather.3.cloned.1.call-update) | async-done | bytes 4194320 | tf_op jit(solution)/shard_map/all_gather | solution.py:119
  217.7 780.5 %while.238 = (s32[]{:T(128)}, f32[4,64,512]{2,1,0:T(8,128)}, f32[4,64,512]{2,1,0:T(8,128)}, f32[8,128,4,512]{3,2,1,0:T(4,128)}, f32[8,4,64,512]{3,2,1,0:T(8,128)...) while((s32[]{:T(128)}, f32[4,64,512]{2,1,0:T(8,128)}, ...), condition=%wide.region_7.8_spmd.clone.clone, body=%wide.region_1.7_spmd.clone.clone.sunk | while | flops 115744832 | bytes 20931168 | solution.py:95
  226.3 83.2 %while.241 = (s32[]{:T(128)}, f32[4,64,512]{2,1,0:T(8,128)S(1)}, f32[4,64,512]{2,1,0:T(8,128)S(1)}, f32[8,16,4,512]{3,2,1,0:T(4,128)}, f32[8,16,4,64]{3,2,1,0:T(...) while((s32[]{:T(128)}, f32[4,64,512]{2,1,0:T(8,128)S(1)}, ...), condition=%wide.region_6.6_spmd.clone, body=%wide.region_2.5_spmd.clone.sunk | while | flops 115744832 | bytes 5921913 | solution.py:80
  323.8 83.2 %while.241 = (s32[]{:T(128)}, f32[4,64,512]{2,1,0:T(8,128)S(1)}, f32[4,64,512]{2,1,0:T(8,128)S(1)}, f32[8,16,4,512]{3,2,1,0:T(4,128)}, f32[8,16,4,64]{3,2,1,0:T(...) while((s32[]{:T(128)}, f32[4,64,512]{2,1,0:T(8,128)S(1)}, ...), condition=%wide.region_6.6_spmd.clone, body=%wide.region_2.5_spmd.clone.sunk | while | flops 115744832 | bytes 5921913 | solution.py:80
  421.2 83.2 %while.241 = (s32[]{:T(128)}, f32[4,64,512]{2,1,0:T(8,128)S(1)}, f32[4,64,512]{2,1,0:T(8,128)S(1)}, f32[8,16,4,512]{3,2,1,0:T(4,128)}, f32[8,16,4,64]{3,2,1,0:T(...) while((s32[]{:T(128)}, f32[4,64,512]{2,1,0:T(8,128)S(1)}, ...), condition=%wide.region_6.6_spmd.clone, body=%wide.region_2.5_spmd.clone.sunk | while | flops 115744832 | bytes 5921913 | solution.py:80
  518.7 83.2 %while.241 = (s32[]{:T(128)}, f32[4,64,512]{2,1,0:T(8,128)S(1)}, f32[4,64,512]{2,1,0:T(8,128)S(1)}, f32[8,16,4,512]{3,2,1,0:T(4,128)}, f32[8,16,4,64]{3,2,1,0:T(...) while((s32[]{:T(128)}, f32[4,64,512]{2,1,0:T(8,128)S(1)}, ...), condition=%wide.region_6.6_spmd.clone, body=%wide.region_2.5_spmd.clone.sunk | while | flops 115744832 | bytes 5921913 | solution.py:80
  616.2 83.2 %while.241 = (s32[]{:T(128)}, f32[4,64,512]{2,1,0:T(8,128)S(1)}, f32[4,64,512]{2,1,0:T(8,128)S(1)}, f32[8,16,4,512]{3,2,1,0:T(4,128)}, f32[8,16,4,64]{3,2,1,0:T(...) while((s32[]{:T(128)}, f32[4,64,512]{2,1,0:T(8,128)S(1)}, ...), condition=%wide.region_6.6_spmd.clone, body=%wide.region_2.5_spmd.clone.sunk | while | flops 115744832 | bytes 5921913 | solution.py:80
  713.7 83.2 %while.241 = (s32[]{:T(128)}, f32[4,64,512]{2,1,0:T(8,128)S(1)}, f32[4,64,512]{2,1,0:T(8,128)S(1)}, f32[8,16,4,512]{3,2,1,0:T(4,128)}, f32[8,16,4,64]{3,2,1,0:T(...) while((s32[]{:T(128)}, f32[4,64,512]{2,1,0:T(8,128)S(1)}, ...), condition=%wide.region_6.6_spmd.clone, body=%wide.region_2.5_spmd.clone.sunk | while | flops 115744832 | bytes 5921913 | solution.py:80
  811.2 83.2 %while.241 = (s32[]{:T(128)}, f32[4,64,512]{2,1,0:T(8,128)S(1)}, f32[4,64,512]{2,1,0:T(8,128)S(1)}, f32[8,16,4,512]{3,2,1,0:T(4,128)}, f32[8,16,4,64]{3,2,1,0:T(...) while((s32[]{:T(128)}, f32[4,64,512]{2,1,0:T(8,128)S(1)}, ...), condition=%wide.region_6.6_spmd.clone, body=%wide.region_2.5_spmd.clone.sunk | while | flops 115744832 | bytes 5921913 | solution.py:80
  908.8 83.2 %while.241 = (s32[]{:T(128)}, f32[4,64,512]{2,1,0:T(8,128)S(1)}, f32[4,64,512]{2,1,0:T(8,128)S(1)}, f32[8,16,4,512]{3,2,1,0:T(4,128)}, f32[8,16,4,64]{3,2,1,0:T(...) while((s32[]{:T(128)}, f32[4,64,512]{2,1,0:T(8,128)S(1)}, ...), condition=%wide.region_6.6_spmd.clone, body=%wide.region_2.5_spmd.clone.sunk | while | flops 115744832 | bytes 5921913 | solution.py:80
  1123.4 274.7 %all-reduce.8.cloned.1.call-done = f32[1024,2048]{1,0:T(8,128)} async-done(((f32[1024,2048]{1,0:T(8,128)}), f32[1024,2048]{1,0:T(8,128)}) %all-reduce.8.cloned.1.call-update) | async-done | bytes 8388624 | tf_op jit(solution)/shard_map/psum | solution.py:178
  1473.6 2958.0 %while.236 = (s32[]{:T(128)}, f32[4,64,512]{2,1,0:T(8,128)S(1)}, f32[4,64,512]{2,1,0:T(8,128)S(1)}, f32[8,128,4,512]{3,2,1,0:T(4,128)}, f32[8,128,4,512]{3,2,1,0...) while((s32[]{:T(128)}, f32[4,64,512]{2,1,0:T(8,128)S(1)}, ...), condition=%wide.region_30.31_spmd, body=%wide.region_14.0_spmd.sunk | while | flops 314950080 | bytes 50768096 | solution.py:95
  1489.9 117.2 %while.239 = (s32[]{:T(128)}, f32[4,64,512]{2,1,0:T(8,128)S(1)}, f32[4,64,512]{2,1,0:T(8,128)S(1)}, f32[8,4,64]{2,1,0:T(4,128)S(1)}, f32[8,4,64,512]{3,2,1,0:T(8...) while((s32[]{:T(128)}, f32[4,64,512]{2,1,0:T(8,128)S(1)}, ...), condition=%wide.region_19.19_spmd.clone.clone, body=%wide.region_15.18_spmd.clone.clone.sunk | while | flops 84529344 | bytes 8700445 | solution.py:80
  1610.3 227.5 %while.240 = (s32[]{:T(128)}, f32[4,64,512]{2,1,0:T(8,128)S(1)}, f32[4,64,512]{2,1,0:T(8,128)S(1)}, f32[8,16,4,512]{3,2,1,0:T(4,128)}, f32[8,16,4,512]{3,2,1,0:T...) while((s32[]{:T(128)}, f32[4,64,512]{2,1,0:T(8,128)S(1)}, ...), condition=%wide.region_29.29_spmd.clone.clone, body=%wide.region_20.28_spmd.clone.clone.sunk | while | flops 230158336 | bytes 13886109 | solution.py:80
  1859.6 117.2 %while.239 = (s32[]{:T(128)}, f32[4,64,512]{2,1,0:T(8,128)S(1)}, f32[4,64,512]{2,1,0:T(8,128)S(1)}, f32[8,4,64]{2,1,0:T(4,128)S(1)}, f32[8,4,64,512]{3,2,1,0:T(8...) while((s32[]{:T(128)}, f32[4,64,512]{2,1,0:T(8,128)S(1)}, ...), condition=%wide.region_19.19_spmd.clone.clone, body=%wide.region_15.18_spmd.clone.clone.sunk | while | flops 84529344 | bytes 8700445 | solution.py:80
  1980.0 227.5 %while.240 = (s32[]{:T(128)}, f32[4,64,512]{2,1,0:T(8,128)S(1)}, f32[4,64,512]{2,1,0:T(8,128)S(1)}, f32[8,16,4,512]{3,2,1,0:T(4,128)}, f32[8,16,4,512]{3,2,1,0:T...) while((s32[]{:T(128)}, f32[4,64,512]{2,1,0:T(8,128)S(1)}, ...), condition=%wide.region_29.29_spmd.clone.clone, body=%wide.region_20.28_spmd.clone.clone.sunk | while | flops 230158336 | bytes 13886109 | solution.py:80
  2229.3 117.2 %while.239 = (s32[]{:T(128)}, f32[4,64,512]{2,1,0:T(8,128)S(1)}, f32[4,64,512]{2,1,0:T(8,128)S(1)}, f32[8,4,64]{2,1,0:T(4,128)S(1)}, f32[8,4,64,512]{3,2,1,0:T(8...) while((s32[]{:T(128)}, f32[4,64,512]{2,1,0:T(8,128)S(1)}, ...), condition=%wide.region_19.19_spmd.clone.clone, body=%wide.region_15.18_spmd.clone.clone.sunk | while | flops 84529344 | bytes 8700445 | solution.py:80
  2349.8 227.5 %while.240 = (s32[]{:T(128)}, f32[4,64,512]{2,1,0:T(8,128)S(1)}, f32[4,64,512]{2,1,0:T(8,128)S(1)}, f32[8,16,4,512]{3,2,1,0:T(4,128)}, f32[8,16,4,512]{3,2,1,0:T...) while((s32[]{:T(128)}, f32[4,64,512]{2,1,0:T(8,128)S(1)}, ...), condition=%wide.region_29.29_spmd.clone.clone, body=%wide.region_20.28_spmd.clone.clone.sunk | while | flops 230158336 | bytes 13886109 | solution.py:80
  2599.0 117.2 %while.239 = (s32[]{:T(128)}, f32[4,64,512]{2,1,0:T(8,128)S(1)}, f32[4,64,512]{2,1,0:T(8,128)S(1)}, f32[8,4,64]{2,1,0:T(4,128)S(1)}, f32[8,4,64,512]{3,2,1,0:T(8...) while((s32[]{:T(128)}, f32[4,64,512]{2,1,0:T(8,128)S(1)}, ...), condition=%wide.region_19.19_spmd.clone.clone, body=%wide.region_15.18_spmd.clone.clone.sunk | while | flops 84529344 | bytes 8700445 | solution.py:80
  2719.4 227.5 %while.240 = (s32[]{:T(128)}, f32[4,64,512]{2,1,0:T(8,128)S(1)}, f32[4,64,512]{2,1,0:T(8,128)S(1)}, f32[8,16,4,512]{3,2,1,0:T(4,128)}, f32[8,16,4,512]{3,2,1,0:T...) while((s32[]{:T(128)}, f32[4,64,512]{2,1,0:T(8,128)S(1)}, ...), condition=%wide.region_29.29_spmd.clone.clone, body=%wide.region_20.28_spmd.clone.clone.sunk | while | flops 230158336 | bytes 13886109 | solution.py:80
  2968.7 117.2 %while.239 = (s32[]{:T(128)}, f32[4,64,512]{2,1,0:T(8,128)S(1)}, f32[4,64,512]{2,1,0:T(8,128)S(1)}, f32[8,4,64]{2,1,0:T(4,128)S(1)}, f32[8,4,64,512]{3,2,1,0:T(8...) while((s32[]{:T(128)}, f32[4,64,512]{2,1,0:T(8,128)S(1)}, ...), condition=%wide.region_19.19_spmd.clone.clone, body=%wide.region_15.18_spmd.clone.clone.sunk | while | flops 84529344 | bytes 8700445 | solution.py:80
  3089.1 227.5 %while.240 = (s32[]{:T(128)}, f32[4,64,512]{2,1,0:T(8,128)S(1)}, f32[4,64,512]{2,1,0:T(8,128)S(1)}, f32[8,16,4,512]{3,2,1,0:T(4,128)}, f32[8,16,4,512]{3,2,1,0:T...) while((s32[]{:T(128)}, f32[4,64,512]{2,1,0:T(8,128)S(1)}, ...), condition=%wide.region_29.29_spmd.clone.clone, body=%wide.region_20.28_spmd.clone.clone.sunk | while | flops 230158336 | bytes 13886109 | solution.py:80
  3338.3 117.2 %while.239 = (s32[]{:T(128)}, f32[4,64,512]{2,1,0:T(8,128)S(1)}, f32[4,64,512]{2,1,0:T(8,128)S(1)}, f32[8,4,64]{2,1,0:T(4,128)S(1)}, f32[8,4,64,512]{3,2,1,0:T(8...) while((s32[]{:T(128)}, f32[4,64,512]{2,1,0:T(8,128)S(1)}, ...), condition=%wide.region_19.19_spmd.clone.clone, body=%wide.region_15.18_spmd.clone.clone.sunk | while | flops 84529344 | bytes 8700445 | solution.py:80
  3458.7 227.5 %while.240 = (s32[]{:T(128)}, f32[4,64,512]{2,1,0:T(8,128)S(1)}, f32[4,64,512]{2,1,0:T(8,128)S(1)}, f32[8,16,4,512]{3,2,1,0:T(4,128)}, f32[8,16,4,512]{3,2,1,0:T...) while((s32[]{:T(128)}, f32[4,64,512]{2,1,0:T(8,128)S(1)}, ...), condition=%wide.region_29.29_spmd.clone.clone, body=%wide.region_20.28_spmd.clone.clone.sunk | while | flops 230158336 | bytes 13886109 | solution.py:80
  3708.0 117.2 %while.239 = (s32[]{:T(128)}, f32[4,64,512]{2,1,0:T(8,128)S(1)}, f32[4,64,512]{2,1,0:T(8,128)S(1)}, f32[8,4,64]{2,1,0:T(4,128)S(1)}, f32[8,4,64,512]{3,2,1,0:T(8...) while((s32[]{:T(128)}, f32[4,64,512]{2,1,0:T(8,128)S(1)}, ...), condition=%wide.region_19.19_spmd.clone.clone, body=%wide.region_15.18_spmd.clone.clone.sunk | while | flops 84529344 | bytes 8700445 | solution.py:80
  3828.4 227.5 %while.240 = (s32[]{:T(128)}, f32[4,64,512]{2,1,0:T(8,128)S(1)}, f32[4,64,512]{2,1,0:T(8,128)S(1)}, f32[8,16,4,512]{3,2,1,0:T(4,128)}, f32[8,16,4,512]{3,2,1,0:T...) while((s32[]{:T(128)}, f32[4,64,512]{2,1,0:T(8,128)S(1)}, ...), condition=%wide.region_29.29_spmd.clone.clone, body=%wide.region_20.28_spmd.clone.clone.sunk | while | flops 230158336 | bytes 13886109 | solution.py:80
  4077.7 117.2 %while.239 = (s32[]{:T(128)}, f32[4,64,512]{2,1,0:T(8,128)S(1)}, f32[4,64,512]{2,1,0:T(8,128)S(1)}, f32[8,4,64]{2,1,0:T(4,128)S(1)}, f32[8,4,64,512]{3,2,1,0:T(8...) while((s32[]{:T(128)}, f32[4,64,512]{2,1,0:T(8,128)S(1)}, ...), condition=%wide.region_19.19_spmd.clone.clone, body=%wide.region_15.18_spmd.clone.clone.sunk | while | flops 84529344 | bytes 8700445 | solution.py:80
  4198.1 227.5 %while.240 = (s32[]{:T(128)}, f32[4,64,512]{2,1,0:T(8,128)S(1)}, f32[4,64,512]{2,1,0:T(8,128)S(1)}, f32[8,16,4,512]{3,2,1,0:T(4,128)}, f32[8,16,4,512]{3,2,1,0:T...) while((s32[]{:T(128)}, f32[4,64,512]{2,1,0:T(8,128)S(1)}, ...), condition=%wide.region_29.29_spmd.clone.clone, body=%wide.region_20.28_spmd.clone.clone.sunk | while | flops 230158336 | bytes 13886109 | solution.py:80
  4675.7 55.0 %reduce-scatter.19.cloned.1.call-done = f32[256,512]{1,0:T(8,128)} async-done(((f32[2048,512]{1,0:T(8,128)}), f32[256,512]{1,0:T(8,128)}) %reduce-scatter.19.cloned.1.call-update) | async-done | bytes 524304 | tf_op jit(solution)/shard_map/reduce_scatter | solution.py:242
  4730.7 91.3 %reduce-scatter.25.cloned.1.call-done = f32[256,1408]{1,0:T(8,128)} async-done(((f32[2048,1408]{1,0:T(8,128)}), f32[256,1408]{1,0:T(8,128)}) %reduce-scatter.25.cloned.1.call-update) | async-done | bytes 1441808 | tf_op jit(solution)/shard_map/reduce_scatter | solution.py:249
  4822.0 91.1 %reduce-scatter.27.cloned.1.call-done = f32[256,1408]{1,0:T(8,128)} async-done(((f32[2048,1408]{1,0:T(8,128)}), f32[256,1408]{1,0:T(8,128)}) %reduce-scatter.27.cloned.1.call-update) | async-done | bytes 1441808 | tf_op jit(solution)/shard_map/reduce_scatter | solution.py:250
  4913.0 91.0 %reduce-scatter.29.cloned.1.call-done = f32[1408,256]{1,0:T(8,128)} async-done(((f32[1408,2048]{1,0:T(8,128)}), f32[1408,256]{1,0:T(8,128)}) %reduce-scatter.29.cloned.1.call-update) | async-done | bytes 1441808 | tf_op jit(solution)/shard_map/reduce_scatter | solution.py:251
  (5823 shorter events, 4285.2 us)
Async XLA Ops:
  7.2 89.6 %copy-start = (bf16[2048,16]{0,1:T(8,128)(2,1)S(1)}, bf16[2048,16]{0,1:T(8,128)(2,1)}, u32[]{:S(2)}) copy-start(bf16[2048,16]{0,1:T(8,128)(2,1)} %param.32) | copy-start | bytes 196612
  7.2 85.9 %all-gather.3.cloned.1.call-start = ((), (), s32[]{:S(2)}) async-start(), calls=%async_computation.10 | async-start | bytes 5242880 | tf_op jit(solution)/shard_map/all_gather | solution.py:119
  7.9 92.3 %copy-start.33 = (bf16[16,256]{1,0:T(8,128)(2,1)S(1)}, bf16[16,256]{1,0:T(8,128)(2,1)}, u32[]{:S(2)}) copy-start(bf16[16,256]{1,0:T(8,128)(2,1)} %param.33) | copy-start | bytes 24580
  7.9 92.3 %copy-start.41 = (f32[256]{0:T(256)S(1)}, f32[256]{0:T(256)}, u32[]{:S(2)}) copy-start(f32[256]{0:T(256)} %param.34) | copy-start | bytes 3076
  8.0 1062.7 %all-gather.5.cloned.1.call-start = ((), (), s32[]{:S(2)}) async-start(), calls=%async_computation.12 | async-start | bytes 5242880 | tf_op jit(solution)/shard_map/all_gather | solution.py:120
  8.7 1389.4 %all-reduce.8.cloned.1.call-start = ((), (), s32[]{:S(2)}) async-start(), calls=%async_computation.13 | async-start | bytes 16777216 | tf_op jit(solution)/shard_map/psum | solution.py:178
  96.7 81.1 %copy-start.28 = (f32[1024]{0:T(1024)}, f32[1024]{0:T(1024)S(1)}, u32[]{:S(2)}) copy-start(f32[1024]{0:T(1024)S(1)} %fusion.192) | copy-start | bytes 12292
  100.2 21.8 copy-start.24
  1020.1 11.9 copy-start.4
  1020.1 11.9 copy-start.35
  1032.0 14.3 copy-start.23
  1046.2 14.1 copy-start.1
  1108.5 3519.2 %reduce-scatter.13.cloned.1.call-start = ((), (), s32[]{:S(2)}) async-start(), calls=%async_computation.11 | async-start | bytes 5242880 | tf_op jit(solution)/shard_map/reduce_scatter | solution.py:160
  1123.3 3512.8 %reduce-scatter.31.cloned.1.call-start = ((), (), s32[]{:S(2)}) async-start(), calls=%async_computation.22 | async-start | bytes 147456
  1398.1 19.0 slice-start.2
  1432.3 10.9 copy-start.32
  1473.6 2962.6 %copy-start.34 = (bf16[16,256]{1,0:T(8,128)(2,1)S(1)}, bf16[16,256]{1,0:T(8,128)(2,1)}, u32[]{:S(2)}) copy-start(bf16[16,256]{1,0:T(8,128)(2,1)} %param.33) | copy-start | bytes 24580
  4431.7 12.6 copy-start.36
  4436.9 15.6 copy-start.21
  4440.2 197.3 %reduce-scatter.21.cloned.1.call-start = ((), (), s32[]{:S(2)}) async-start(), calls=%async_computation.17 | async-start | bytes 147456 | tf_op jit(solution)/shard_map/reduce_scatter | solution.py:243
  4444.3 193.3 %reduce-scatter.23.cloned.1.call-start = ((), (), s32[]{:S(2)}) async-start(), calls=%async_computation.18 | async-start | bytes 4718592 | tf_op jit(solution)/shard_map/reduce_scatter | solution.py:247
  4452.5 185.1 %reduce-scatter.17.cloned.1.call-start = ((), (), s32[]{:S(2)}) async-start(), calls=%async_computation.15 | async-start | bytes 4718592 | tf_op jit(solution)/shard_map/reduce_scatter | solution.py:241
  4472.5 203.2 %reduce-scatter.15.cloned.1.call-start = ((), (), s32[]{:S(2)}) async-start(), calls=%async_computation.14 | async-start | bytes 4718592 | tf_op jit(solution)/shard_map/reduce_scatter | solution.py:240
  4492.8 237.9 %reduce-scatter.19.cloned.1.call-start = ((), (), s32[]{:S(2)}) async-start(), calls=%async_computation.16 | async-start | bytes 4718592 | tf_op jit(solution)/shard_map/reduce_scatter | solution.py:242
  4503.3 318.6 %reduce-scatter.25.cloned.1.call-start = ((), (), s32[]{:S(2)}) async-start(), calls=%async_computation.19 | async-start | bytes 12976128 | tf_op jit(solution)/shard_map/reduce_scatter | solution.py:249
  4515.3 397.7 %reduce-scatter.27.cloned.1.call-start = ((), (), s32[]{:S(2)}) async-start(), calls=%async_computation.20 | async-start | bytes 12976128 | tf_op jit(solution)/shard_map/reduce_scatter | solution.py:250
  4527.5 476.5 %reduce-scatter.29.cloned.1.call-start = ((), (), s32[]{:S(2)}) async-start(), calls=%async_computation.21 | async-start | bytes 12976128 | tf_op jit(solution)/shard_map/reduce_scatter | solution.py:251
  4549.6 12.8 copy-start.15
  4562.4 13.4 copy-start.17
  4575.8 14.4 copy-start.8
  4575.8 14.4 copy-start.22
  4590.2 36.2 copy-start.26
  (32 other events, 234.9 us)
Sparse Core Ops, SparseCore 0:
  9.6 83.4 all-gather.2
  94.6 79.2 all-gather.4
  1108.6 289.5 all-reduce.7
  1400.3 75.7 reduce-scatter.12
  4440.3 32.6 reduce-scatter.30
  4476.5 33.5 reduce-scatter.20
  4514.0 51.1 reduce-scatter.22
  4569.1 51.4 reduce-scatter.16
  4624.5 51.1 reduce-scatter.14
  4679.5 51.1 reduce-scatter.18
  4734.8 87.1 reduce-scatter.24
  4825.9 87.1 reduce-scatter.26
  4917.1 86.8 reduce-scatter.28
where the time goes:
time: 5100 us; the launch traced here: 5010 us
  matrix products  2080 us (41%)
  local copies, waits for them, and re-layouts  1160 us (23%)
  other arithmetic  985 us (19%)
  waiting for transfers between devices  725 us (14%)
    dot_general x256, matrix products, piece_step(): jnp.einsum('cso,sio->csi', query_rows, key_slot_state, precision=HIGH_PRE...  357 us
    dot_general x256, matrix products, piece_step(): jnp.einsum('thd,jhd->htj', query_rows, key_row_block, precision=HIGH_PREC...  286 us
    psum x1, waiting for transfers between devices, local(): grad_normed_mlp = lax.psum(partial_grad, 'mp')  275 us
    dot_general x256, matrix products, piece_step(): jnp.einsum('eoq,eon->oqn', carried_state, value_row_block, precision=HIGH...  261 us
    dynamic_slice x448, local copies, waits for them, and re-layouts, slot_block(): states, output_rows = lax.scan(piece_step, states, pieces)  258 us
    dot_general x192, matrix products, piece_step(): jnp.einsum('lwe,wez->lwz', attention_probabilities * jnp.exp(running_tota...  236 us
    dynamic_update_slice x320, other arithmetic, slot_block(): states, output_rows = lax.scan(piece_step, states, pieces)  221 us
    dot_general x256, matrix products, piece_step(): jnp.einsum('eoq,eon->oqn', carried_state, key_row_block, precision=HIGH_P...  204 us

commit v1 on v0

v1 whole, which is shorter than its diff:
```python
import functools
import math

import jax
import jax.numpy as jnp
from jax import lax
from jax.experimental import pallas as pl
from jax.experimental.pallas import tpu as pltpu
from jax.sharding import PartitionSpec as P

HEADS = 4
CHUNK = 128
LANES = 128
EPS = 1e-06
GATE_NORM = 8.0
RANGE_LIMIT = 60.0
HIGH_PRECISION = lax.Precision.HIGHEST
NN = (((1,), (0,)), ((), ()))
TN = (((0,), (0,)), ((), ()))
NT = (((1,), (1,)), ((), ()))


def low(values):
    return values.astype(jnp.bfloat16)


def product(left, right, dims=NN):
    return lax.dot_general(left, right, dims, preferred_element_type=jnp.float32)


def fine(left, right, dims=NN):
    return lax.dot_general(
        left, right, dims, precision=HIGH_PRECISION, preferred_element_type=jnp.float32
    )


def silu_slope(raw):
    sigmoid = jax.nn.sigmoid(raw)
    return sigmoid * (1.0 + raw * (1.0 - sigmoid))


def sigmoid(raw):
    return 1.0 / (1.0 + jnp.exp(-raw))


def iota(shape, axis):
    return lax.broadcasted_iota(jnp.int32, shape, axis)


def column_of(row):
    size = row.shape[1]
    eye = iota((size, size), 0) == iota((size, size), 1)
    return jnp.sum(jnp.where(eye, row, 0.0), axis=1, keepdims=True)


def row_of(column):
    size = column.shape[0]
    eye = iota((size, size), 0) == iota((size, size), 1)
    return jnp.sum(jnp.where(eye, column, 0.0), axis=0, keepdims=True)


def causal_mask(size):
    return iota((size, size), 0) >= iota((size, size), 1)


def decays(rank, forget, bias):
    logits = fine(rank, forget) + bias
    log_decay = (jnp.minimum(logits, 0.0) - jnp.log1p(jnp.exp(-jnp.abs(logits)))) / GATE_NORM
    size = rank.shape[0]
    total = fine(causal_mask(size).astype(jnp.float32), log_decay)
    return logits, log_decay, total


def direct_factors(total):
    size = total.shape[0]
    middle = 0.5 * total[size - 1 :, :]
    return causal_mask(size), jnp.exp(total - middle), jnp.exp(middle - total)


def level_factors(total, level):
    size = total.shape[0]
    half = jnp.left_shift(1, level)
    row, column = iota((size, size), 0), iota((size, size), 1)
    row_span = jnp.right_shift(row, level + 1)
    mask = (
        (row_span == jnp.right_shift(column, level + 1))
        & (jnp.bitwise_and(row, half) != 0)
        & (jnp.bitwise_and(column, half) == 0)
    )
    pick = column == jnp.left_shift(row_span, level + 1) + half - 1
    middle = fine(pick.astype(jnp.float32), total)
    return (
        mask,
        jnp.exp(jnp.minimum(total - middle, 0.0)),
        jnp.exp(jnp.minimum(middle - total, 0.0)),
    )


def over_levels(total, first, term):
    size = total.shape[0]
    eye = iota((size, size), 0) == iota((size, size), 1)
    ones = jnp.ones_like(total)
    start = first((eye, ones, ones))
    count = size.bit_length() - 1

    def body(level, running):
        return jax.tree.map(jnp.add, running, term(level_factors(total, level)))

    return lax.fori_loop(0, count, body, start)


def forward_kernel(
    q_ref,
    k_ref,
    v_ref,
    rank_ref,
    forget_ref,
    bias_ref,
    gain_ref,
    a_ref,
    o_ref,
    soft_ref,
    kept_ref,
    key_state,
    value_state,
    score_ref,
    mix_ref,
):
    @pl.when(pl.program_id(0) == 0)
    def _():
        key_state[...] = jnp.zeros_like(key_state)
        value_state[...] = jnp.zeros_like(value_state)

    kept_ref[0, 0] = key_state[...]
    kept_ref[0, 1] = value_state[...]
    size = q_ref.shape[0]
    slots = bias_ref.shape[1]
    scale = 1.0 / math.sqrt(q_ref.shape[1])
    q_raw, k_raw = q_ref[...], k_ref[...]
    q, k, v = low(q_raw * sigmoid(q_raw)), low(k_raw * sigmoid(k_raw)), low(v_ref[...])
    _, log_decay, total = decays(rank_ref[...], forget_ref[...], bias_ref[...])
    fresh = 1.0 - jnp.exp(log_decay)
    last = total[size - 1 :, :]
    from_start = jnp.exp(total)
    direct = product(q, k, NT)
    carried = from_start * product(q, low(key_state[...]), NT)
    narrow = jnp.max(-last) <= RANGE_LIMIT

    def intra_scores(factors):
        mask, late, early = factors
        return late * fine(jnp.where(mask, direct, 0.0), early * fresh)

    def soft(scores):
        return jax.nn.softmax(scores, axis=-1)

    def intra_mix(weights):
        def term(factors):
            mask, late, early = factors
            return jnp.where(mask, fine(weights * late, early * fresh, NT), 0.0)

        return term

    @pl.when(narrow)
    def _():
        factors = direct_factors(total)
        scores = (intra_scores(factors) + carried) * scale
        score_ref[...] = scores
        mix_ref[...] = intra_mix(soft(scores))(factors)

    @pl.when(jnp.logical_not(narrow))
    def _():
        scores = (over_levels(total, intra_scores, intra_scores) + carried) * scale
        score_ref[...] = scores
        term = intra_mix(soft(scores))
        mix_ref[...] = over_levels(total, term, term)

    scores = score_ref[...]
    weights = soft(scores)
    soft_ref[:, :slots] = scores
    soft_ref[:, slots:] = weights
    out = product(low(weights * from_start), low(value_state[...])) + product(
        low(mix_ref[...]), v
    )
    o_ref[...] = out
    a_ref[...] = low(
        out * lax.rsqrt(jnp.mean(out * out, axis=-1, keepdims=True) + EPS) * gain_ref[...]
    )
    to_end = low(jnp.exp(last - total) * fresh)
    keep = column_of(jnp.exp(last))
    key_state[...] = keep * key_state[...] + product(to_end, k, TN)
    value_state[...] = keep * value_state[...] + product(to_end, v, TN)


def backward_kernel(
    q_ref,
    k_ref,
    v_ref,
    rank_ref,
    o_ref,
    soft_ref,
    kept_ref,
    da_ref,
    forget_ref,
    bias_ref,
    gain_ref,
    draw_ref,
    dforget_ref,
    dbias_ref,
    dgain_ref,
    key_back,
    value_back,
    dp_ref,
    da_part_ref,
    mix_ref,
    early_ref,
):
    @pl.when(pl.program_id(0) == 0)
    def _():
        key_back[...] = jnp.zeros_like(key_back)
        value_back[...] = jnp.zeros_like(value_back)
        dforget_ref[...] = jnp.zeros_like(dforget_ref)
        dbias_ref[...] = jnp.zeros_like(dbias_ref)
        dgain_ref[...] = jnp.zeros_like(dgain_ref)

    size, width = q_ref.shape
    slots = bias_ref.shape[1]
    scale = 1.0 / math.sqrt(width)
    q_raw, k_raw = q_ref[...], k_ref[...]
    q_sig, k_sig = sigmoid(q_raw), sigmoid(k_raw)
    q, k, v = low(q_raw * q_sig), low(k_raw * k_sig), low(v_ref[...])
    rank, forget = rank_ref[...], forget_ref[...]
    logits, log_decay, total = decays(rank, forget, bias_ref[...])
    decay = jnp.exp(log_decay)
    fresh = 1.0 - decay
    last = total[size - 1 :, :]
    from_start = jnp.exp(total)
    to_end = jnp.exp(last - total)
    narrow = jnp.max(-last) <= RANGE_LIMIT
    scores, weights = soft_ref[:, :slots], soft_ref[:, slots:]
    key_start, value_start = kept_ref[0, 0], kept_ref[0, 1]
    key_end, value_end = key_back[...], value_back[...]

    out, da = o_ref[...], da_ref[...].astype(jnp.float32)
    inverse = lax.rsqrt(jnp.mean(out * out, axis=-1, keepdims=True) + EPS)
    unit = out * inverse
    dgain_ref[...] += jnp.sum(da * unit, axis=0, keepdims=True)
    scaled = da * gain_ref[...]
    do = low(inverse * (scaled - unit * jnp.mean(scaled * unit, axis=-1, keepdims=True)))

    direct = product(q, k, NT)
    dmix = product(do, v, NT)
    dp_carried = from_start * product(do, low(value_start), NT)

    def intra_dp(factors):
        mask, late, early = factors
        return late * fine(jnp.where(mask, dmix, 0.0), early * fresh)

    def back_scores(dp):
        return weights * (dp - jnp.sum(weights * dp, axis=-1, keepdims=True))

    def intra_back(ds):
        def term(factors):
            mask, late, early = factors
            ds_late, p_late, factor = ds * late, weights * late, early * fresh
            return (
                jnp.where(mask, fine(ds_late, factor, NT), 0.0),
                jnp.where(mask, fine(p_late, factor, NT), 0.0),
                early
                * (
                    fine(jnp.where(mask, direct, 0.0), ds_late, TN)
                    + fine(jnp.where(mask, dmix, 0.0), p_late, TN)
                ),
            )

        return term

    def store(dp, parts):
        dp_ref[...] = dp
        da_part_ref[...], mix_ref[...], early_ref[...] = parts

    @pl.when(narrow)
    def _():
        factors = direct_factors(total)
        dp = intra_dp(factors) + dp_carried
        store(dp, intra_back(back_scores(dp) * scale)(factors))

    @pl.when(jnp.logical_not(narrow))
    def _():
        dp = over_levels(total, intra_dp, intra_dp) + dp_carried
        term = intra_back(back_scores(dp) * scale)
        store(dp, over_levels(total, term, term))

    dp = dp_ref[...]
    ds = back_scores(dp)
    ds_scaled = ds * scale
    ddirect, mix, early_sum = low(da_part_ref[...]), low(mix_ref[...]), early_ref[...]
    late_sum = ds * scores + weights * dp
    end_sum = to_end * (product(k, low(key_end), NT) + product(v, low(value_end), NT))
    carry = low(to_end * fresh)
    ds_start, p_start = low(ds_scaled * from_start), low(weights * from_start)

    dq = product(ddirect, k) + product(ds_start, low(key_start))
    dk = product(ddirect, q, TN) + product(carry, low(key_end))
    dv = product(mix, do, TN) + product(carry, low(value_end))
    draw_ref[:, :width] = low(dq * (q_sig * (1.0 + q_raw * (1.0 - q_sig))))
    draw_ref[:, width : 2 * width] = low(dk * (k_sig * (1.0 + k_raw * (1.0 - k_sig))))
    draw_ref[:, 2 * width : 3 * width] = low(dv)

    keep = jnp.exp(last)
    through = keep * row_of(
        jnp.sum(key_start * key_end + value_start * value_end, axis=1, keepdims=True)
    )
    after = (iota((size, size), 0) <= iota((size, size), 1)).astype(jnp.float32)
    before = (iota((size, size), 0) > iota((size, size), 1)).astype(jnp.float32)
    dlog = (
        fine(after, late_sum - fresh * early_sum)
        + fine(before, fresh * end_sum)
        + through
        - decay * (early_sum + end_sum)
    )
    dlogits = dlog * (1.0 / (1.0 + jnp.exp(logits))) / GATE_NORM
    dbias_ref[...] += jnp.sum(dlogits, axis=0, keepdims=True)
    dforget_ref[...] += fine(rank, dlogits, TN)
    draw_ref[:, 3 * width :] = low(fine(dlogits, forget, NT))

    keep_column = column_of(keep)
    key_back[...] = keep_column * key_end + product(ds_start, q, TN)
    value_back[...] = keep_column * value_end + product(p_start, do, TN)


def piece_specs(width, chunk, order):
    parts = [
        pl.BlockSpec((chunk, width), functools.partial(lambda part, i: (order(i), part), part))
        for part in range(3)
    ]
    rank = pl.BlockSpec((chunk, LANES), lambda i: (order(i), 3 * width // LANES))
    return parts + [rank]


def whole(shape):
    return pl.BlockSpec(shape, lambda i: (0,) * len(shape))


def mixer_forward(raw, forget, bias, gain):
    length, slots, width = raw.shape[0], bias.shape[1], gain.shape[1]
    steps = length // CHUNK

    def order(i):
        return i

    def rows(size):
        return pl.BlockSpec((CHUNK, size), lambda i: (order(i), 0))

    return pl.pallas_call(
        forward_kernel,
        grid=(steps,),
        in_specs=piece_specs(width, CHUNK, order)
        + [whole(forget.shape), whole(bias.shape), whole(gain.shape)],
        out_specs=(
            rows(width),
            rows(width),
            rows(2 * slots),
            pl.BlockSpec((1, 2, slots, width), lambda i: (i, 0, 0, 0)),
        ),
        out_shape=(
            jax.ShapeDtypeStruct((length, width), jnp.bfloat16),
            jax.ShapeDtypeStruct((length, width), jnp.float32),
            jax.ShapeDtypeStruct((length, 2 * slots), jnp.float32),
            jax.ShapeDtypeStruct((steps, 2, slots, width), jnp.float32),
        ),
        scratch_shapes=[
            pltpu.VMEM((slots, width), jnp.float32),
            pltpu.VMEM((slots, width), jnp.float32),
            pltpu.VMEM((CHUNK, slots), jnp.float32),
            pltpu.VMEM((CHUNK, CHUNK), jnp.float32),
        ],
        cost_estimate=pl.CostEstimate(
            flops=2 * length * width * 1024, bytes_accessed=length * width * 20, transcendentals=0
        ),
        name="mixer_forward",
    )(raw, raw, raw, raw, forget, bias, gain)


def mixer_backward(raw, out, soft, kept, da, forget, bias, gain):
    length, slots, width = raw.shape[0], bias.shape[1], gain.shape[1]
    steps = length // CHUNK

    def order(i):
        return steps - 1 - i

    def rows(size):
        return pl.BlockSpec((CHUNK, size), lambda i: (order(i), 0))

    return pl.pallas_call(
        backward_kernel,
        grid=(steps,),
        in_specs=piece_specs(width, CHUNK, order)
        + [
            rows(width),
            rows(2 * slots),
            pl.BlockSpec((1, 2, slots, width), lambda i: (order(i), 0, 0, 0)),
            rows(width),
            whole(forget.shape),
            whole(bias.shape),
            whole(gain.shape),
        ],
        out_specs=(
            rows(3 * width + LANES),
            whole(forget.shape),
            whole(bias.shape),
            whole(gain.shape),
        ),
        out_shape=(
            jax.ShapeDtypeStruct((length, 3 * width + LANES), jnp.bfloat16),
            jax.ShapeDtypeStruct(forget.shape, jnp.float32),
            jax.ShapeDtypeStruct(bias.shape, jnp.float32),
            jax.ShapeDtypeStruct(gain.shape, jnp.float32),
        ),
        scratch_shapes=[
            pltpu.VMEM((slots, width), jnp.float32),
            pltpu.VMEM((slots, width), jnp.float32),
            pltpu.VMEM((CHUNK, slots), jnp.float32),
            pltpu.VMEM((CHUNK, CHUNK), jnp.float32),
            pltpu.VMEM((CHUNK, CHUNK), jnp.float32),
            pltpu.VMEM((CHUNK, slots), jnp.float32),
        ],
        cost_estimate=pl.CostEstimate(
            flops=4 * length * width * 1024, bytes_accessed=length * width * 24, transcendentals=0
        ),
        name="mixer_backward",
    )(raw, raw, raw, raw, out, soft, kept, da, forget, bias, gain)


def inverse_rms(values):
    return lax.rsqrt(jnp.mean(values * values, axis=-1, keepdims=True) + EPS)


def norm_back(values, inverse, gain, grad):
    unit = values * inverse
    scaled = gain * grad
    grad_values = inverse * (scaled - unit * jnp.mean(scaled * unit, axis=-1, keepdims=True))
    return grad_values, jnp.sum(grad * unit, axis=0)


def local(
    tokens,
    valid,
    attn_gain,
    w_query,
    w_key,
    w_value,
    w_rank,
    w_forget,
    forget_bias,
    head_gain,
    w_out,
    mlp_gain,
    w_gate,
    w_up,
    w_down,
    cotangent,
):
    width = w_query.shape[0]
    head_size = width // HEADS
    slots = forget_bias.shape[0] // HEADS
    ranks = w_rank.shape[1]
    rows = tokens.shape[0]
    shards, shard = lax.axis_size("mp"), lax.axis_index("mp")
    copies = shards // HEADS
    own_width = width // shards
    head, part = shard // copies, shard % copies
    begin = shard * rows

    def own_rows(values):
        return lax.dynamic_slice_in_dim(values, begin, rows, 0)

    def head_columns(values, size):
        return lax.dynamic_slice_in_dim(values, head * size, size, values.ndim - 1)

    def own_part(values):
        if copies == 1:
            return values
        pieces = [
            lax.dynamic_slice_in_dim(values, i * head_size + part * own_width, own_width, 1)
            for i in range(values.shape[1] // head_size)
        ]
        return jnp.concatenate(pieces, axis=1)

    counted = (part == 0).astype(jnp.float32)
    own_mask = ((begin + jnp.arange(rows)) < valid[0])[:, None]
    own_cotangent = jnp.where(own_mask, cotangent, jnp.zeros_like(cotangent))
    gathered = lax.all_gather(tokens, "mp", axis=0, tiled=True)
    grad_output = lax.all_gather(own_cotangent, "mp", axis=0, tiled=True)

    w_inputs = jnp.concatenate(
        [head_columns(w, head_size) for w in (w_query, w_key, w_value)]
        + [jnp.pad(w_rank, ((0, 0), (0, LANES - ranks)))],
        axis=1,
    )
    forget = jnp.pad(
        head_columns(w_forget.astype(jnp.float32), slots), ((0, LANES - ranks), (0, 0))
    )
    bias = head_columns(forget_bias, slots)[None]
    gain = head_gain[None]

    resid = gathered.astype(jnp.float32)
    normed = low(resid * inverse_rms(resid) * attn_gain)
    raw = product(normed, w_inputs)
    a_head, mixed, soft, kept = mixer_forward(raw, forget, bias, gain)
    a_all = lax.all_gather(own_part(a_head), "mp", axis=1, tiled=True)
    hidden = resid + product(a_all, w_out)
    mlp_normed = low(hidden * inverse_rms(hidden) * mlp_gain)
    gate = product(mlp_normed, w_gate)
    up = product(mlp_normed, w_up)
    activated = jax.nn.silu(gate)
    inner = low(activated * up)
    grad_inner = product(grad_output, w_down, NT)
    grad_gate_low = low(grad_inner * up * silu_slope(gate))
    grad_up_low = low(grad_inner * activated)
    partial = product(grad_gate_low, w_gate, NT) + product(grad_up_low, w_up, NT)
    grad_normed = lax.psum_scatter(
        low(partial), "mp", scatter_dimension=0, tiled=True
    ).astype(jnp.float32)

    own_hidden = own_rows(hidden)
    grad_hidden, part_mlp_gain = norm_back(
        own_hidden, inverse_rms(own_hidden), mlp_gain, grad_normed
    )
    grad_hidden = grad_hidden + own_cotangent.astype(jnp.float32)
    grad_hidden_all = lax.all_gather(low(grad_hidden), "mp", axis=0, tiled=True)
    w_out_rows = lax.dynamic_slice_in_dim(w_out, head * head_size, head_size, 0)
    grad_a = product(grad_hidden_all, w_out_rows, NT)
    draw, part_forget, part_bias, part_head_gain = mixer_backward(
        raw, mixed, soft, kept, grad_a, forget, bias, gain
    )
    draw_inputs = own_part(draw[:, : 3 * head_size])
    draw_rank = draw[:, 3 * head_size :]
    if copies > 1:
        draw_rank = low(draw_rank.astype(jnp.float32) * counted)
        w_own = jnp.concatenate([own_part(w_inputs[:, : 3 * head_size]), w_inputs[:, 3 * head_size :]], axis=1)
        draw = jnp.concatenate([draw_inputs, draw_rank], axis=1)
    else:
        w_own = w_inputs
    partial_input = product(draw, w_own, NT)
    grad_input = lax.psum_scatter(
        low(partial_input), "mp", scatter_dimension=0, tiled=True
    ).astype(jnp.float32)
    own_resid = tokens.astype(jnp.float32)
    grad_resid, part_attn_gain = norm_back(
        own_resid, inverse_rms(own_resid), attn_gain, grad_input
    )
    grad_tokens = grad_hidden + grad_resid

    mlp_own = lax.psum_scatter(
        low(product(inner, w_down)), "mp", scatter_dimension=0, tiled=True
    ).astype(jnp.float32)
    output = low(jnp.where(own_mask, own_hidden + mlp_own, 0.0))

    def dp_sum(values, axis):
        return lax.psum_scatter(
            low(values), "dp", scatter_dimension=axis, tiled=True
        ).astype(jnp.float32)

    sum_down = dp_sum(product(inner, grad_output, TN), 1)
    sum_gate = dp_sum(product(mlp_normed, grad_gate_low, TN), 0)
    sum_up = dp_sum(product(mlp_normed, grad_up_low, TN), 0)
    own_grad_hidden = lax.dynamic_slice_in_dim(
        grad_hidden_all, shard * own_width, own_width, 1
    )
    sum_wout = dp_sum(product(a_all, own_grad_hidden, TN), 0)
    sum_inputs = dp_sum(product(normed, draw_inputs, TN), 0)
    sum_query, sum_key, sum_value = (
        sum_inputs[:, i * own_width : (i + 1) * own_width] for i in range(3)
    )
    part_rank = product(draw_rank[:, :ranks], normed, TN)

    def place(values):
        spread = jnp.zeros((values.shape[0], HEADS * slots), jnp.float32)
        return lax.dynamic_update_slice_in_dim(spread, values * counted, head * slots, 1)

    small = lax.psum(
        (
            part_rank,
            place(part_forget[:ranks]),
            place(part_bias),
            part_head_gain * counted,
            part_attn_gain[None],
            part_mlp_gain[None],
        ),
        ("dp", "mp"),
    )
    replicas, replica = lax.axis_size("dp"), lax.axis_index("dp")

    def own_slice(values):
        size = values.shape[1] // replicas
        return lax.dynamic_slice_in_dim(values, replica * size, size, 1)

    sum_rank, sum_forget, sum_bias, sum_head_gain, sum_attn_gain, sum_mlp_gain = (
        own_slice(values) for values in small
    )
    return (
        output,
        grad_tokens,
        sum_attn_gain[0],
        sum_query,
        sum_key,
        sum_value,
        sum_rank.T,
        sum_forget,
        sum_bias[0],
        sum_head_gain[0],
        sum_wout,
        sum_mlp_gain[0],
        sum_gate,
        sum_up,
        sum_down,
    )


def solution(mesh):
    return jax.shard_map(
        local,
        mesh=mesh,
        in_specs=(
            P(("dp", "mp"), None),
            P("dp"),
            P(),
            P(),
            P(),
            P(),
            P(),
            P(),
            P(),
            P(),
            P(),
            P(),
            P(None, "mp"),
            P(None, "mp"),
            P("mp", None),
            P(("dp", "mp"), None),
        ),
        out_specs=(
            P(("dp", "mp"), None),
            P(("dp", "mp"), None),
            P("dp"),
            P("dp", "mp"),
            P("dp", "mp"),
            P("dp", "mp"),
            P("dp", None),
            P(None, "dp"),
            P("dp"),
            P("dp"),
            P("dp", "mp"),
            P("dp"),
            P("dp", "mp"),
            P("dp", "mp"),
            P("mp", "dp"),
        ),
        check_vma=False,
    )
```

time: 5100 us -> 1090 us (0.21); the launches traced: 5010 us -> 1080 us
  matrix products: 2080 us -> 169 us
  local copies, waits for them, and re-layouts: 1160 us -> 21.9 us
  other arithmetic: 985 us -> 29.6 us
    dot_general x1818 -> x16, matrix products: 2070 us -> 169 us  [product(): lax.dot_general(left, right, dims, preferred_element_type=jnp.float32)]
    dynamic_update_slice x552 -> x2, local copies, waits for them, and re-layouts: 345 us -> 0.33 us  [place(): lax.dynamic_update_slice_in_dim(spread, values * counted, head * slots, 1)]
    dynamic_slice x490 -> x5, local copies, waits for them, and re-layouts: 326 us -> 8.8 us  [the longest x2 7 us: head_columns(): return lax.dynamic_slice_in_dim(values, head * size, size, values.ndim - 1)]
    mul x513 -> x0, other arithmetic: 252 us -> none  [the longest x256 133 us: piece_step(): jnp.where(causal, jnp.exp(jnp.where(causal, spread, 0.0)), 0.0)]
    reduce_sum x198 -> x5, other arithmetic: 254 us -> 10.1 us  [the longest x3 5.32 us: inverse_rms(): return lax.rsqrt(jnp.mean(values * values, axis=-1, keepdims=True) + EPS)]
    dynamic_update_slice x320 -> x0, other arithmetic: 221 us -> none  [slot_block(): states, output_rows = lax.scan(piece_step, states, pieces)]
    squeeze x304 -> x2, local copies, waits for them, and re-layouts: 175 us -> 1.17 us  [the longest x1 0.59 us: local(): sum_bias[0]]
    all_gather x2 -> x4, waiting for transfers between devices: 81.7 us -> 244 us  [the longest x1 77.2 us: local(): a_all = lax.all_gather(own_part(a_head), 'mp', axis=1, tiled=True)]
where the time goes in v1:
time: 1090 us; the launch traced here: 1080 us
  waiting for transfers between devices  754 us (69%)
  matrix products  169 us (16%)
  blocking collectives  46.2 us (4%)
  Pallas kernels  44.9 us (4%)
  other arithmetic  29.6 us (3%)
  local copies, waits for them, and re-layouts  21.9 us (2%)
  between operations  15.3 us (1%)
    reduce_scatter x5, waiting for transfers between devices, dp_sum(): lax.psum_scatter(low(values), 'dp', scatter_dimension=axis, tiled=True)  201 us
    dot_general x16, matrix products, product(): lax.dot_general(left, right, dims, preferred_element_type=jnp.float32)  169 us
    psum x1, waiting for transfers between devices, local(): lax.psum((part_rank, place(part_forget[:ranks]), place(part_bias), part_h...  127 us
    reduce_scatter x1, waiting for transfers between devices, local(): lax.psum_scatter(low(partial_input), 'mp', scatter_dimension=0, tiled=True)  77.3 us
    all_gather x1, waiting for transfers between devices, local(): a_all = lax.all_gather(own_part(a_head), 'mp', axis=1, tiled=True)  77.2 us
    all_gather x1, waiting for transfers between devices, local(): gathered = lax.all_gather(tokens, 'mp', axis=0, tiled=True)  74.9 us
    reduce_scatter x1, waiting for transfers between devices, local(): lax.psum_scatter(low(partial), 'mp', scatter_dimension=0, tiled=True)  73.6 us
    all_gather x1, waiting for transfers between devices, local(): grad_hidden_all = lax.all_gather(low(grad_hidden), 'mp', axis=0, tiled=True)  48.5 us
  transfers between devices with their start and end apart: 13, of which 12 were waited for; matrix products, arithmetic and copies ran while one was open for 14% of the time, Pallas kernels for 3%

profile of v1, /device:TPU:0, one launch (start us, length us, event | category | flops | bytes accessed | tf_op | source)
XLA Modules:
  0.0 1081.5 jit_solution(1453910265591842194)
XLA Ops:
  12.9 5.3 constant_dynamic-slice_fusion.5
  18.2 74.9 %all-gather.5.cloned.1.call-done = bf16[1024,2048]{1,0:T(8,128)(2,1)} async-done(((bf16[256,2048]{1,0:T(8,128)(2,1)}), bf16[1024,2048]{1,0:T(8,128)(2,1)}) %all-gather.5.cloned.1.call-update) | async-done | bytes 4194320 | tf_op jit(solution)/shard_map/all_gather | solution.py:492
  96.5 12.9 %fusion.31.q_ref.k_ref.v_ref.rank_ref = f32[1024,1664]{1,0:T(8,128)} fusion(bf16[2048,16]{1,0:T(8,128)(2,1)S(1)} %copy.32, bf16[2048,512]{1,0:T(8,128)(2,1)} %get-tuple-element.50, bf16[2048,512]{1,0:T(8,128)(2,1)} %get-tuple-element.51, bf16[2048,512]{1,0:T(8,128)(2,1)S(1)} %constant_dynamic-slice_fusion.7, bf16[1024,2048]{1,0:T(8,128)(2,1)S(1)} %copy-done.7, ...), kind=kOutput, calls=%fused_computation.75 | convolution fusion | flops 7021789184 | bytes 17379328 | tf_op jit(solution)/shard_map/dot_general | solution.py:28
  109.4 16.4 %mixer_forward.1 = (bf16[1024,512]{1,0:T(8,128)(2,1)}, f32[1024,512]{1,0:T(8,128)}, f32[1024,128]{1,0:T(8,128)}, f32[8,2,64,512]{3,2,1,0:T(8,128)}) custom-call(f32[1024,1664]{1,0:T(8,128)} %fusion.31.q_ref.k_ref.v_ref.rank_ref, f32[1024,1664]{1,0:T(8,128)} %fusion.31.q_ref.k_ref.v_ref.rank_ref, f32[1024,1664]{1,0:T(8,128)} %fusion.31.q_ref.k_ref.v_ref.rank_ref, ...), custom_call_target="tpu_custom_call" | custom-call | flops 1073741824 | bytes 10485760 | tf_op jit(solution)/shard_map/mixer_forward/pallas_call | solution.py:354
  127.9 77.2 %all-gather.7.cloned.1.call-done = bf16[1024,2048]{1,0:T(8,128)(2,1)} async-done(((bf16[1024,512]{1,0:T(8,128)(2,1)}), bf16[1024,2048]{1,0:T(8,128)(2,1)}) %all-gather.7.cloned.1.call-update) | async-done | bytes 4194320 | tf_op jit(solution)/shard_map/all_gather | solution.py:510
  205.2 13.3 %multiply_reduce_fusion = (f32[1024]{0:T(1024)S(1)}, f32[1024,2048]{1,0:T(8,128)S(1)}) fusion(bf16[1024,2048]{1,0:T(8,128)(2,1)} %all-gather.7.cloned.1.call-done, bf16[2048,2048]{1,0:T(8,128)(2,1)} %param.26, bf16[1024,2048]{1,0:T(8,128)(2,1)} %all-gather.5.cloned.1.call-done), kind=kOutput, calls=%fused_computation.10 | convolution fusion | flops 8598322176 | bytes 25169920 | tf_op jit(solution)/shard_map/dot_general | solution.py:28
  222.8 11.9 %fusion.38 = f32[1024,1408]{1,0:T(8,128)} fusion(bf16[1024,2048]{1,0:T(8,128)(2,1)S(1)} %multiply_convert_fusion, bf16[2048,1408]{1,0:T(8,128)(2,1)} %param.28), kind=kOutput, calls=%fused_computation.78 | convolution fusion | flops 5905580032 | bytes 15728640 | tf_op jit(solution)/shard_map/dot_general | solution.py:28
  234.7 8.5 fusion.39
  243.2 43.4 %all-gather.9.cloned.1.call-done = bf16[1024,2048]{1,0:T(8,128)(2,1)} async-done(((bf16[256,2048]{1,0:T(8,128)(2,1)}), bf16[1024,2048]{1,0:T(8,128)(2,1)}) %all-gather.9.cloned.1.call-update) | async-done | bytes 4194320 | tf_op jit(solution)/shard_map/all_gather | solution.py:493
  286.6 15.9 %multiply_convert_fusion.1 = (bf16[1024,1408]{1,0:T(8,128)(2,1)S(1)}, bf16[1024,1408]{1,0:T(8,128)(2,1)S(1)}, bf16[1024,1408]{1,0:T(8,128)(2,1)}) fusion(f32[1024,1408]{1,0:T(8,128)} %fusion.38, f32[1024,1408]{1,0:T(8,128)} %fusion.39, bf16[1024,2048]{1,0:T(8,128)(2,1)} %all-gather.9.cloned.1.call-done, bf16[1408,2048]{1,0:T(8,128)(2,1)} %param.30), kind=kOutput, calls=%fused_computation.16 | convolution fusion | flops 5927206912 | bytes 30146560 | tf_op jit(solution)/shard_map/dot_general | solution.py:28
  302.5 10.8 fusion.40
  313.4 10.9 %add_convert_fusion = bf16[1024,2048]{1,0:T(8,128)(2,1)} fusion(f32[1024,2048]{1,0:T(8,128)S(1)} %fusion.40, bf16[1024,1408]{1,0:T(8,128)(2,1)S(1)} %get-tuple-element.40, bf16[2048,1408]{1,0:T(8,128)(2,1)} %param.29), kind=kOutput, calls=%fused_computation.8 | convolution fusion | flops 5909774336 | bytes 21233664 | tf_op jit(solution)/shard_map/dot_general | solution.py:28
  326.2 73.6 %reduce-scatter.11.cloned.1.call-done = bf16[256,2048]{1,0:T(8,128)(2,1)} async-done(((bf16[1024,2048]{1,0:T(8,128)(2,1)}), bf16[256,2048]{1,0:T(8,128)(2,1)}) %reduce-scatter.11.cloned.1.call-update) | async-done | bytes 1048592 | tf_op jit(solution)/shard_map/reduce_scatter | solution.py:521
  406.1 11.1 %convolution_convert_fusion.2 = bf16[2048,1408]{1,0:T(8,128)(2,1)} fusion(bf16[1024,2048]{1,0:T(8,128)(2,1)} %copy-done.6, bf16[1024,1408]{1,0:T(8,128)(2,1)} %copy-done.18), kind=kOutput, calls=%fused_computation.13 | convolution fusion | flops 5908463616 | bytes 12845056 | tf_op jit(solution)/shard_map/dot_general | solution.py:28
  417.3 11.1 %convolution_convert_fusion.1 = bf16[2048,1408]{1,0:T(8,128)(2,1)} fusion(bf16[1024,2048]{1,0:T(8,128)(2,1)} %copy-done.6, bf16[1024,1408]{1,0:T(8,128)(2,1)} %copy-done.19), kind=kOutput, calls=%fused_computation.12 | convolution fusion | flops 5908463616 | bytes 12845056 | tf_op jit(solution)/shard_map/dot_general | solution.py:28
  428.4 10.5 convolution_convert_fusion
  439.0 48.5 %all-gather.11.cloned.1.call-done = bf16[1024,2048]{1,0:T(8,128)(2,1)} async-done(((bf16[256,2048]{1,0:T(8,128)(2,1)}), bf16[1024,2048]{1,0:T(8,128)(2,1)}) %all-gather.11.cloned.1.call-update) | async-done | bytes 4194320 | tf_op jit(solution)/shard_map/all_gather | solution.py:530
  487.4 6.6 fusion.21.da_ref
  494.0 28.5 %mixer_backward.1 = (bf16[1024,1664]{1,0:T(8,128)(2,1)}, f32[128,64]{1,0:T(8,128)}, f32[1,64]{1,0:T(1,128)}, f32[1,512]{1,0:T(1,128)}) custom-call(f32[1024,1664]{1,0:T(8,128)} %fusion.31.q_ref.k_ref.v_ref.rank_ref, f32[1024,1664]{1,0:T(8,128)} %fusion.31.q_ref.k_ref.v_ref.rank_ref, f32[1024,1664]{1,0:T(8,128)} %fusion.31.q_ref.k_ref.v_ref.rank_ref, ...), custom_call_target="tpu_custom_call" | custom-call | flops 2147483648 | bytes 12582912 | tf_op jit(solution)/shard_map/mixer_backward/pallas_call | solution.py:394
  526.8 6.4 convolution_convert_fusion.6
  533.3 12.2 %convolution_convert_fusion.4 = bf16[1024,2048]{1,0:T(8,128)(2,1)} fusion(bf16[1024,1664]{1,0:T(8,128)(2,1)} %get-tuple-element.27, bf16[2048,16]{1,0:T(8,128)(2,1)} %copy-done.10, bf16[2048,512]{1,0:T(8,128)(2,1)} %get-tuple-element.50, bf16[2048,512]{1,0:T(8,128)(2,1)} %get-tuple-element.51, bf16[2048,512]{1,0:T(8,128)(2,1)S(1)} %copy-done.9), kind=kOutput, calls=%fused_computation.21 | convolution fusion | flops 7015497728 | bytes 13959168 | tf_op jit(solution)/shard_map/dot_general | solution.py:28
  545.6 11.0 %convolution_convert_fusion.5 = bf16[1024,2048]{1,0:T(8,128)(2,1)} fusion(bf16[1024,1408]{1,0:T(8,128)(2,1)} %get-tuple-element.42, bf16[1408,2048]{1,0:T(8,128)(2,1)} %param.30), kind=kOutput, calls=%fused_computation.22 | convolution fusion | flops 5907677184 | bytes 12845056 | tf_op jit(solution)/shard_map/dot_general | solution.py:28
  556.6 12.1 %convolution_convert_fusion.3 = bf16[2048,1536]{1,0:T(8,128)(2,1)} fusion(bf16[1024,1664]{1,0:T(8,128)(2,1)} %get-tuple-element.27, bf16[1024,2048]{1,0:T(8,128)(2,1)} %all-gather.5.cloned.1.call-done, f32[2048]{0:T(1024)S(1)} %copy-done.13, f32[1024]{0:T(1024)S(1)} %copy-done.15), kind=kOutput, calls=%fused_computation.14 | convolution fusion | flops 6453985280 | bytes 13643776 | tf_op jit(solution)/shard_map/dot_general | solution.py:28
  572.6 38.2 %reduce-scatter.21.cloned.1.call-done = bf16[256,1408]{1,0:T(8,128)(2,1)} async-done(((bf16[2048,1408]{1,0:T(8,128)(2,1)}), bf16[256,1408]{1,0:T(8,128)(2,1)}) %reduce-scatter.21.cloned.1.call-update) | async-done | bytes 720912 | tf_op jit(solution)/shard_map/reduce_scatter | solution.py:560
  613.1 60.0 %reduce-scatter.23.cloned.1.call-done = bf16[1408,256]{1,0:T(8,128)(2,1)} async-done(((bf16[1408,2048]{1,0:T(8,128)(2,1)}), bf16[1408,256]{1,0:T(8,128)(2,1)}) %reduce-scatter.23.cloned.1.call-update) | async-done | bytes 720912 | tf_op jit(solution)/shard_map/reduce_scatter | solution.py:560
  676.5 127.2 %all-reduce.5.cloned.1.call-done = f32[16,2048]{1,0:T(8,128)} async-done(((f32[16,2048]{1,0:T(8,128)}), f32[16,2048]{1,0:T(8,128)}) %all-reduce.5.cloned.1.call-update) | async-done | bytes 131088 | tf_op jit(solution)/shard_map/psum | solution.py:581
  805.0 42.0 %reduce-scatter.17.cloned.1.call-done = bf16[256,512]{1,0:T(8,128)(2,1)} async-done(((bf16[2048,512]{1,0:T(8,128)(2,1)}), bf16[256,512]{1,0:T(8,128)(2,1)}) %reduce-scatter.17.cloned.1.call-update) | async-done | bytes 262160 | tf_op jit(solution)/shard_map/reduce_scatter | solution.py:560
  848.8 77.3 %reduce-scatter.13.cloned.1.call-done = bf16[256,2048]{1,0:T(8,128)(2,1)} async-done(((bf16[1024,2048]{1,0:T(8,128)(2,1)}), bf16[256,2048]{1,0:T(8,128)(2,1)}) %reduce-scatter.13.cloned.1.call-update) | async-done | bytes 1048592 | tf_op jit(solution)/shard_map/reduce_scatter | solution.py:545
  928.2 46.2 %all-reduce.2 = (f32[1,2048]{1,0:T(1,128)S(1)}, f32[16,256]{1,0:T(8,128)S(1)}, f32[1,256]{1,0:T(1,128)S(1)}, f32[1,512]{1,0:T(1,128)S(1)}, f32[1,2048]{1,0:T(1,128)S(1)}) all-reduce(f32[1,2048]{1,0:T(1,128)S(1)} %bitcast.39, f32[16,256]{1,0:T(8,128)S(1)} %dynamic_update_slice.6, ...), channel_id=1, replica_groups=mesh['dp'=8,'mp'=4] {'dp','mp'}, use_global_device_ids=true, to_apply=%region_10.11 | all-reduce | flops 8960 | bytes 71680 | tf_op jit(solution)/shard_map/psum | solution.py:581
  977.3 29.3 %reduce-scatter.9.cloned.1.call-done = bf16[256,2048]{1,0:T(8,128)(2,1)} async-done(((bf16[1024,2048]{1,0:T(8,128)(2,1)}), bf16[256,2048]{1,0:T(8,128)(2,1)}) %reduce-scatter.9.cloned.1.call-update) | async-done | bytes 1048592 | tf_op jit(solution)/shard_map/reduce_scatter | solution.py:554
  1006.7 4.4 fusion.13
  1011.1 61.1 %reduce-scatter.15.cloned.1.call-done = bf16[256,1536]{1,0:T(8,128)(2,1)} async-done(((bf16[2048,1536]{1,0:T(8,128)(2,1)}), bf16[256,1536]{1,0:T(8,128)(2,1)}) %reduce-scatter.15.cloned.1.call-update) | async-done | bytes 786448 | tf_op jit(solution)/shard_map/reduce_scatter | solution.py:560
  (109 shorter events, 47.5 us)
Async XLA Ops:
  7.2 85.9 %all-gather.5.cloned.1.call-start = ((), (), s32[]{:S(2)}) async-start(), calls=%async_computation.8 | async-start | bytes 5242880 | tf_op jit(solution)/shard_map/all_gather | solution.py:492
  7.9 197.3 %all-gather.7.cloned.1.call-start = ((), (), s32[]{:S(2)}) async-start(), calls=%async_computation.9 | async-start | bytes 5242880 | tf_op jit(solution)/shard_map/all_gather | solution.py:510
  9.1 87.2 %copy-start.10 = (bf16[2048,16]{1,0:T(8,128)(2,1)}, bf16[2048,16]{1,0:T(8,128)(2,1)S(1)}, u32[]{:S(2)}) copy-start(bf16[2048,16]{1,0:T(8,128)(2,1)S(1)} %copy.32) | copy-start | bytes 196612
  12.9 83.4 %copy-start.8 = (bf16[2048,512]{1,0:T(8,128)(2,1)}, bf16[2048,512]{1,0:T(8,128)(2,1)S(1)}, u32[]{:S(2)}) copy-start(bf16[2048,512]{1,0:T(8,128)(2,1)S(1)} %constant_dynamic-slice_fusion.7) | copy-start | bytes 6291460
  18.2 78.2 %copy-start.12 = (f32[2048]{0:T(1024)S(1)}, f32[2048]{0:T(1024)}, u32[]{:S(2)}) copy-start(f32[2048]{0:T(1024)} %param.18) | copy-start | bytes 24580
  96.3 13.1 %copy-start.14 = (f32[1024]{0:T(1024)}, f32[1024]{0:T(1024)S(1)}, u32[]{:S(2)}) copy-start(f32[1024]{0:T(1024)S(1)} %add_rsqrt_fusion.1) | copy-start | bytes 12292
  109.4 17.1 %copy-start.4 = (bf16[256,2048]{1,0:T(8,128)(2,1)S(1)}, bf16[256,2048]{1,0:T(8,128)(2,1)}, u32[]{:S(2)}) copy-start(bf16[256,2048]{1,0:T(8,128)(2,1)} %param.31) | copy-start | bytes 3145732
  125.8 160.8 %all-gather.9.cloned.1.call-start = ((), (), s32[]{:S(2)}) async-start(), calls=%async_computation.11 | async-start | bytes 5242880 | tf_op jit(solution)/shard_map/all_gather | solution.py:493
  127.7 90.9 %copy-start.11 = (f32[2048]{0:T(1024)S(1)}, f32[2048]{0:T(1024)}, u32[]{:S(2)}) copy-start(f32[2048]{0:T(1024)} %param.27) | copy-start | bytes 24580
  127.7 272.0 %reduce-scatter.11.cloned.1.call-start = ((), (), s32[]{:S(2)}) async-start(), calls=%async_computation.12 | async-start | bytes 5242880 | tf_op jit(solution)/shard_map/reduce_scatter | solution.py:521
  218.5 4.3 copy-start.2
  218.6 16.1 %slice-start = ((s8[5767168]{0:T(1024)(128)(4,1)}), s8[4194304]{0:T(1024)(128)(4,1)S(1)}, s32[]{:S(2)}) async-start(s8[5767168]{0:T(1024)(128)(4,1)} %bitcast.44), calls=%async_computation.21 | async-start | bytes 8388608
  222.8 11.9 %copy-start.6 = (bf16[1024,2048]{1,0:T(8,128)(2,1)}, bf16[1024,2048]{1,0:T(8,128)(2,1)S(1)}, u32[]{:S(2)}) copy-start(bf16[1024,2048]{1,0:T(8,128)(2,1)S(1)} %multiply_convert_fusion) | copy-start | bytes 12582916
  222.8 11.9 %slice-start.1 = ((s8[5767168]{0:T(1024)(128)(4,1)}), s8[1572864]{0:T(1024)(128)(4,1)S(1)}, s32[]{:S(2)}) async-start(s8[5767168]{0:T(1024)(128)(4,1)} %bitcast.44), calls=%async_computation.22 | async-start | bytes 3145728
  302.5 10.8 %copy-start.18 = (bf16[1024,1408]{1,0:T(8,128)(2,1)}, bf16[1024,1408]{1,0:T(8,128)(2,1)S(1)}, u32[]{:S(2)}) copy-start(bf16[1024,1408]{1,0:T(8,128)(2,1)S(1)} %get-tuple-element.41) | copy-start | bytes 8650756
  302.5 10.8 %copy-start.19 = (bf16[1024,1408]{1,0:T(8,128)(2,1)}, bf16[1024,1408]{1,0:T(8,128)(2,1)S(1)}, u32[]{:S(2)}) copy-start(bf16[1024,1408]{1,0:T(8,128)(2,1)S(1)} %get-tuple-element.40) | copy-start | bytes 8650756
  324.3 163.1 %all-gather.11.cloned.1.call-start = ((), (), s32[]{:S(2)}) async-start(), calls=%async_computation.13 | async-start | bytes 5242880 | tf_op jit(solution)/shard_map/all_gather | solution.py:530
  406.0 164.2 %reduce-scatter.19.cloned.1.call-start = ((), (), s32[]{:S(2)}) async-start(), calls=%async_computation.18 | async-start | bytes 6488064 | tf_op jit(solution)/shard_map/reduce_scatter | solution.py:560
  417.2 193.5 %reduce-scatter.21.cloned.1.call-start = ((), (), s32[]{:S(2)}) async-start(), calls=%async_computation.19 | async-start | bytes 6488064 | tf_op jit(solution)/shard_map/reduce_scatter | solution.py:560
  428.4 244.7 %reduce-scatter.23.cloned.1.call-start = ((), (), s32[]{:S(2)}) async-start(), calls=%async_computation.20 | async-start | bytes 6488064 | tf_op jit(solution)/shard_map/reduce_scatter | solution.py:560
  438.9 364.8 %all-reduce.5.cloned.1.call-start = ((), (), s32[]{:S(2)}) async-start(), calls=%async_computation.16 | async-start | bytes 262144 | tf_op jit(solution)/shard_map/psum | solution.py:581
  494.0 28.5 %copy-start.13 = (f32[2048]{0:T(1024)S(1)}, f32[2048]{0:T(1024)}, u32[]{:S(2)}) copy-start(f32[2048]{0:T(1024)} %param.18) | copy-start | bytes 24580
  494.0 28.5 %copy-start.15 = (f32[1024]{0:T(1024)S(1)}, f32[1024]{0:T(1024)}, u32[]{:S(2)}) copy-start(f32[1024]{0:T(1024)} %copy-done.14) | copy-start | bytes 12292
  526.8 6.6 copy-start.9
  526.8 320.2 %reduce-scatter.17.cloned.1.call-start = ((), (), s32[]{:S(2)}) async-start(), calls=%async_computation.17 | async-start | bytes 2359296 | tf_op jit(solution)/shard_map/reduce_scatter | solution.py:560
  533.3 392.8 %reduce-scatter.13.cloned.1.call-start = ((), (), s32[]{:S(2)}) async-start(), calls=%async_computation.14 | async-start | bytes 5242880 | tf_op jit(solution)/shard_map/reduce_scatter | solution.py:545
  545.5 461.1 %reduce-scatter.9.cloned.1.call-start = ((), (), s32[]{:S(2)}) async-start(), calls=%async_computation.10 | async-start | bytes 5242880 | tf_op jit(solution)/shard_map/reduce_scatter | solution.py:554
  556.6 515.7 %reduce-scatter.15.cloned.1.call-start = ((), (), s32[]{:S(2)}) async-start(), calls=%async_computation.15 | async-start | bytes 7077888 | tf_op jit(solution)/shard_map/reduce_scatter | solution.py:560
  568.8 107.6 %copy-start.17 = (f32[1,64]{1,0:T(1,128)S(1)}, f32[1,64]{1,0:T(1,128)}, u32[]{:S(2)}) copy-start(f32[1,64]{1,0:T(1,128)} %get-tuple-element.29) | copy-start | bytes 772
  572.6 355.6 %copy-start.16 = (f32[1,512]{1,0:T(1,128)S(1)}, f32[1,512]{1,0:T(1,128)}, u32[]{:S(2)}) copy-start(f32[1,512]{1,0:T(1,128)} %get-tuple-element.30) | copy-start | bytes 6148
  572.6 434.1 %copy-start.5 = (bf16[256,2048]{1,0:T(8,128)(2,1)S(1)}, bf16[256,2048]{1,0:T(8,128)(2,1)}, u32[]{:S(2)}) copy-start(bf16[256,2048]{1,0:T(8,128)(2,1)} %reduce-scatter.11.cloned.1.call-done) | copy-start | bytes 3145732
  1006.7 67.9 %copy-start.1 = (f32[256]{0:T(256)S(1)}, f32[256]{0:T(256)}, u32[]{:S(2)}) copy-start(f32[256]{0:T(256)} %param.24) | copy-start | bytes 3076
  (3 other events, 8.1 us)
Sparse Core Ops, SparseCore 0:
  9.6 83.4 all-gather.4
  125.9 79.2 all-gather.6
  207.3 79.2 all-gather.8
  324.4 75.2 reduce-scatter.10
  406.1 81.2 all-gather.10
  490.7 57.4 reduce-scatter.18
  551.7 59.0 reduce-scatter.20
  614.2 58.8 reduce-scatter.22
  679.2 124.3 all-reduce.4
  806.8 40.1 reduce-scatter.16
  849.3 76.7 reduce-scatter.12
  928.3 78.3 reduce-scatter.8
  1010.0 62.1 reduce-scatter.14
